TPU v7x, 32 devices: a whole 2x2x4 slice. The times are simulated.
32 devices in a mesh: space: 4 (over y, x), vel: 8 (over z, core).
Axes of the slice: x: 2, y: 2, z: 4, core: 2. Of those that a mesh axis runs over, the one named last changes fastest.
Arguments:
- distribution: float32 [256, 64, 4096], P('space', None, 'vel'), may hold values from -6 to 6
- inverse_jacobian: float32 [256, 3, 3], P('space'), may hold values from -1 to 1
- density: float32 [256, 64], P('space'), may hold values from 1 to 10
- collision_blocks: float32 [32, 6, 128, 128], replicated, may hold values from -0.21875 to 0.21875
- block_columns: int32 [32, 6], replicated, may hold values from 0 to 31, as said below
- send_lists: int32 [4, 4, 48], P('space'), may hold values from 0 to 383, as said below
- exterior_faces: int32 [256, 6], P('space'), may hold values from 0 to 576, as said below
Outputs:
- advanced: float32 [256, 64, 4096], P('space', None, 'vel')
Inputs may be any that keep to these rules, and one draw needn't show every extreme that they name: `block_columns`: each row b lists 6 different block columns, the first being b itself. send_lists[q, p] holds different faces (6 e + s, e local to q) in its first slots and 0 in the slots after them; send_lists[p, p] is all 0. Every used slot is read by exactly one face of partition p, and slots after the used ones are read by none. `exterior_faces`: an entry below 384 names a face 6 e + s of the partition's own elements; 384 + q * 48 + j names slot j of the list partition q sends to this partition; 576 marks a wall, whose exterior trace is zero. Exactly 32 faces of each partition are walls.
All inputs are finite; a program needn't handle non-finite values.
Results may differ from a plain program's by a relative error of at most 0.0003.
Values sent between devices are 32-bit elements; how exact they have to be, the bound alone decides.
No kernel may reach another device: no remote copies, remote signals or barrier semaphores. Data moves between devices by JAX's collectives and lax.ppermute only.
A program may use at most 256 MiB of HBM per device.

v0:
```python
import functools

import jax
import jax.numpy as jnp
import numpy as np
from jax import lax
from jax.experimental import pallas as pl
from jax.experimental.pallas import tpu as pltpu
from jax.sharding import PartitionSpec as P


VG = 16
SIDE = 4
FACES = 6
FACE_NODES = 16
LANES = 128

TIME_STEP = 0.03
LIFT_SCALE = 6.0


MIB = 1024 * 1024


def lagrange_derivative():
    points = np.array([-1.0, -1.0 / np.sqrt(5.0), 1.0 / np.sqrt(5.0), 1.0])
    barycentric = np.ones(4)
    for column in range(4):
        for second in range(4):
            if second != column:
                barycentric[column] = barycentric[column] / (points[column] - points[second])
    matrix = np.zeros((4, 4))
    for row_node in range(4):
        for col_node in range(4):
            if row_node != col_node:
                matrix[row_node, col_node] = (
                    barycentric[col_node]
                    / barycentric[row_node]
                    / (points[row_node] - points[col_node])
                )
        matrix[row_node, row_node] = -np.sum(matrix[row_node])
    return matrix


def derivative_parts():
    single = lagrange_derivative()
    identity = np.eye(4)
    stacked = np.concatenate(
        [
            np.kron(np.kron(single, identity), identity),
            np.kron(np.kron(identity, single), identity),
            np.kron(np.kron(identity, identity), single),
        ],
        0,
    ).astype(np.float32)
    high = stacked.astype(jnp.bfloat16)
    low = (stacked - high.astype(np.float32)).astype(jnp.bfloat16)
    return np.concatenate([high, high, low], 1)


def lift_parts():
    nodes = SIDE**3
    place = np.zeros((nodes, 3, 2, FACE_NODES), np.float32)
    for node in range(nodes):
        index = (node // 16, node // 4 % 4, node % 4)
        for direction in range(3):
            others = [index[d] for d in range(3) if d != direction]
            if index[direction] == 0:
                place[node, direction, 0, others[0] * 4 + others[1]] = 1.0
            if index[direction] == SIDE - 1:
                place[node, direction, 1, others[0] * 4 + others[1]] = 1.0
    place = place.reshape(nodes, 6 * FACE_NODES).astype(jnp.bfloat16)
    return np.concatenate([place, place], 1)


def shell():
    nodes = np.ndindex(SIDE, SIDE, SIDE)
    return [index for index in nodes if 0 in index]


SHELL = len(shell())
SHELL_MAIN = SHELL // 32 * 32
SHELL_ROWS = -(-SHELL // 8) * 8


def turned(index, flip):
    return tuple(SIDE - 1 - i if f else i for i, f in zip(index, flip))


def pack_parts():
    rows = {index: row for row, index in enumerate(shell())}
    pack = np.zeros((SHELL_ROWS, 3, 2, 2, FACE_NODES), np.float32)
    for direction in range(3):
        for first, second, a, b in np.ndindex(2, 2, SIDE, SIDE):
            where = list(turned((a, b), (first, second)))
            where.insert(direction, 0)
            pack[rows[tuple(where)], direction, first, second, a * SIDE + b] = 1.0
    pack = pack.reshape(SHELL_ROWS, -1).astype(jnp.bfloat16)
    return np.concatenate([pack, pack], 1)


def spread_parts():
    spread = np.zeros((SIDE, SIDE, SIDE, 2, 2, 2, SHELL_ROWS), np.float32)
    for flip in np.ndindex(2, 2, 2):
        for row, index in enumerate(shell()):
            spread[turned(index, flip) + flip + (row,)] = 1.0
    spread = spread.reshape(SIDE**3, -1).astype(jnp.bfloat16)
    return np.concatenate([spread, spread], 1)


def grid_velocities(first_id, amount):
    velocity_id = first_id + jnp.arange(amount, dtype=jnp.int32)
    components = [velocity_id // (VG * VG), velocity_id // VG % VG, velocity_id % VG]
    return jnp.stack(
        [3.0 * ((2.0 * component.astype(jnp.float32) + 1.0) / VG - 1.0) for component in components]
    )


def halves(value):
    high = value.astype(jnp.bfloat16)
    return high, (value - high.astype(jnp.float32)).astype(jnp.bfloat16)


def speeds_of(jacobian_ref, element, velocity):
    result = []
    for direction in range(3):
        base = element * 9 + direction * 3
        result.append(
            jacobian_ref[base] * velocity[0:1]
            + jacobian_ref[base + 1] * velocity[1:2]
            + jacobian_ref[base + 2] * velocity[2:3]
        )
    return result


def lifted(fluxes, speeds, lift):
    pieces = []
    for flux, speed in zip(fluxes, speeds):
        inward = speed > 0.0
        pieces.append(jnp.where(inward, flux, 0.0))
        pieces.append(jnp.where(inward, 0.0, flux))
    high, low = halves(jnp.concatenate(pieces, 0))
    return jnp.dot(lift, jnp.concatenate([high, low], 0), preferred_element_type=jnp.float32)


def signs(speeds):
    return [(jnp.where(s > 0.0, 1.0, 0.0), jnp.where(s > 0.0, 0.0, 1.0)) for s in speeds]


def packed(fluxes, speeds, pack):
    masks = signs(speeds)
    pieces = []
    for direction, flux in enumerate(fluxes):
        first, second = [masks[d] for d in range(3) if d != direction]
        pieces += [flux * (a * b) for a in first for b in second]
    high, low = halves(jnp.concatenate(pieces, 0))
    return jnp.dot(pack, jnp.concatenate([high, low], 0), preferred_element_type=jnp.float32)


def spread_out(rows, speeds, spread):
    masks = signs(speeds)
    pieces = [rows * (a * b * c) for a in masks[0] for b in masks[1] for c in masks[2]]
    high, low = halves(jnp.concatenate(pieces, 0))
    return jnp.dot(spread, jnp.concatenate([high, low], 0), preferred_element_type=jnp.float32)


def shell_rows(flux_ref, tail_ref, owned, element):
    for row in range(SHELL - SHELL_MAIN):
        at = owned * SHELL_MAIN + row * owned + element
        tail_ref[row : row + 1, :] = flux_ref[0, pl.ds(at, 1), :]
    for row in range(SHELL - SHELL_MAIN, tail_ref.shape[0]):
        tail_ref[row : row + 1, :] = jnp.zeros((1, tail_ref.shape[1]), jnp.float32)
    start = pl.multiple_of(element * SHELL_MAIN, SHELL_MAIN)
    return lambda lanes: jnp.concatenate(
        [flux_ref[0, pl.ds(start, SHELL_MAIN), lanes], tail_ref[:, lanes]], 0
    )


def own_flow(value, speeds, derivative):
    high, low = halves(value)
    slopes = jnp.dot(
        derivative, jnp.concatenate([high, low, high], 0), preferred_element_type=jnp.float32
    )
    node = lax.broadcasted_iota(jnp.int32, value.shape, 0)
    count = value.shape[0]
    total = None
    for direction in range(3):
        speed = speeds[direction]
        place = (node >> (4 - 2 * direction)) & 3
        side = jnp.where(speed > 0.0, 0, SIDE - 1)
        edge = jnp.where(place == side, LIFT_SCALE * jnp.abs(speed), 0.0)
        term = speed * slopes[direction * count : (direction + 1) * count] + edge * value
        total = term if total is None else total + term
    return -total


def lane_chunks(width):
    step = 2 * LANES if width % (2 * LANES) == 0 else LANES
    return [pl.ds(start, step) for start in range(0, width, step)]


def whole(space=pltpu.VMEM):
    return pl.BlockSpec(memory_space=space)


def params(mebibytes):
    return pltpu.CompilerParams(vmem_limit_bytes=mebibytes * MIB)


def cost(flops, moved):
    return pl.CostEstimate(flops=int(flops), bytes_accessed=int(moved), transcendentals=0)


def faces_kernel(cap, others, send_ref, *refs):
    value_ref = refs[0]
    change_ref = refs[1] if len(refs) > others + 2 else None
    table_ref, out_refs = refs[-1 - others], refs[len(refs) - others :]
    elements = value_ref.shape[0]
    surface = surface_nodes()

    def rows(element, start, stop):
        value = value_ref[element, start:stop, :]
        if change_ref is None:
            return value
        at = surface.index(start)
        return value + TIME_STEP * change_ref[element, at : at + stop - start, :]

    def build(element, carry):
        face = element * FACES
        table_ref[face] = rows(element, 0, 16)
        table_ref[face + 1] = rows(element, 48, 64)
        for i in range(SIDE):
            to = slice(4 * i, 4 * i + 4)
            table_ref[face + 2, to, :] = rows(element, 16 * i, 16 * i + 4)
            table_ref[face + 3, to, :] = rows(element, 16 * i + 12, 16 * i + 16)
        for m in range(FACE_NODES):
            to = slice(m, m + 1)
            table_ref[face + 4, to, :] = rows(element, 4 * m, 4 * m + 1)
            table_ref[face + 5, to, :] = rows(element, 4 * m + 3, 4 * m + 4)
        return carry

    lax.fori_loop(0, elements, build, 0)
    for number, out_ref in enumerate(out_refs):

        def pick(slot, carry, number=number, out_ref=out_ref):
            out_ref[slot] = table_ref[send_ref[number * cap + slot]]
            return carry

        lax.fori_loop(0, cap, pick, 0)


def faces(values, send_ids, others, cap):
    elements, _, width = values[0].shape
    out_shape = [jax.ShapeDtypeStruct((FACES * elements, FACE_NODES, width), jnp.float32)]
    out_shape += [jax.ShapeDtypeStruct((cap, FACE_NODES, width), jnp.float32)] * others
    moved = sum(value.size for value in values)
    moved += width * FACE_NODES * (FACES * elements + others * cap)
    return pl.pallas_call(
        functools.partial(faces_kernel, cap, others),
        out_shape=out_shape,
        in_specs=[whole(pltpu.SMEM)] + [whole()] * len(values),
        out_specs=[whole()] * (1 + others),
        compiler_params=params(44),
        cost_estimate=cost(0, 8 * moved),
        name="faces",
    )(send_ids, *values)


def inflow_kernel(scale, lookup_ref, jacobian_ref, velocity_ref, lift_ref, table_ref, in_ref, out_ref):
    local = table_ref.shape[0]
    remote = in_ref.shape[0]
    elements = local // FACES
    velocity = velocity_ref[...]

    def one(element, carry):
        speeds = speeds_of(jacobian_ref, element, velocity)
        fluxes = []
        for direction in range(3):
            traces = []
            for side in range(2):
                index = lookup_ref[element * FACES + 2 * direction + side]
                near = table_ref[jnp.minimum(index, local - 1)]
                far = in_ref[jnp.clip(index - local, 0, remote - 1)]
                far = jnp.where(index < local + remote, far, 0.0)
                traces.append(jnp.where(index < local, near, far))
            speed = speeds[direction]
            fluxes.append(
                (LIFT_SCALE * jnp.abs(speed)) * jnp.where(speed > 0.0, traces[0], traces[1])
            )
        if scale is None:
            owned = elements // out_ref.shape[0]
            owner, own = lax.div(element, owned), lax.rem(element, owned)
            rows = packed(fluxes, speeds, lift_ref[...])
            start = pl.multiple_of(own * SHELL_MAIN, SHELL_MAIN)
            out_ref[owner, pl.ds(start, SHELL_MAIN), :] = rows[:SHELL_MAIN]
            for row in range(SHELL_MAIN, SHELL):
                at = owned * SHELL_MAIN + (row - SHELL_MAIN) * owned + own
                out_ref[owner, pl.ds(at, 1), :] = rows[row : row + 1]
        else:
            out_ref[element] = scale * lifted(fluxes, speeds, lift_ref[...])
        return carry

    lax.fori_loop(0, elements, one, 0)


def inflow(table, incoming, lookup, jacobian, velocity, lift, scale, owners):
    width = table.shape[2]
    elements = table.shape[0] // FACES
    shape = (elements, SIDE**3, width)
    if scale is None:
        shape = (owners, elements // owners * SHELL, width)
    moved = table.size + incoming.size + np.prod(shape)
    return pl.pallas_call(
        functools.partial(inflow_kernel, scale),
        out_shape=jax.ShapeDtypeStruct(shape, jnp.float32),
        in_specs=[whole(pltpu.SMEM)] * 2 + [whole()] * 4,
        out_specs=whole(),
        compiler_params=params(36),
        cost_estimate=cost(0, 8 * moved),
        name="inflow",
    )(lookup, jacobian, velocity, lift, table, incoming)


def guess_kernel(
    owned, jacobian_ref, velocity_ref, derivative_ref, spread_ref, value_ref, flux_ref, out_ref, tail_ref
):
    element = pl.program_id(0)
    shell_of = shell_rows(flux_ref, tail_ref, owned, lax.rem(element, owned))
    for lanes in lane_chunks(value_ref.shape[2]):
        value = value_ref[0, :, lanes]
        speeds = speeds_of(jacobian_ref, element, velocity_ref[:, lanes])
        entering = spread_out(shell_of(lanes), speeds, spread_ref[...])
        flow = own_flow(value, speeds, derivative_ref[...]) + entering
        out_ref[0, :, lanes] = value + TIME_STEP * flow


def guess(value, flux, jacobian, velocity, derivative, spread):
    elements, nodes, width = value.shape
    owners, rows, _ = flux.shape
    owned = elements // owners
    return pl.pallas_call(
        functools.partial(guess_kernel, owned),
        grid=(elements,),
        out_shape=jax.ShapeDtypeStruct(value.shape, jnp.float32),
        in_specs=[
            whole(pltpu.SMEM),
            whole(),
            whole(),
            whole(),
            pl.BlockSpec((1, nodes, width), lambda e: (e, 0, 0)),
            pl.BlockSpec((1, rows, width), lambda e: (e // owned, 0, 0)),
        ],
        out_specs=pl.BlockSpec((1, nodes, width), lambda e: (e, 0, 0)),
        scratch_shapes=[pltpu.VMEM((SHELL_ROWS - SHELL_MAIN, width), jnp.float32)],
        compiler_params=params(16),
        cost_estimate=cost(2 * 256 * 192 * value.size // 64, 4 * (2 * value.size + flux.size)),
        name="guess",
    )(jacobian, velocity, derivative, spread, value, flux)


def stage_kernel(
    order_ref,
    jacobian_ref,
    velocity_ref,
    derivative_ref,
    spread_ref,
    value_ref,
    flux_ref,
    change_ref,
    first_ref,
    rest_ref,
    tail_ref,
):
    element = pl.program_id(1)
    shell_of = shell_rows(flux_ref, tail_ref, pl.num_programs(1), element)
    for lanes in lane_chunks(value_ref.shape[3]):
        value = value_ref[0, 0, :, lanes]
        speeds = speeds_of(jacobian_ref, element, velocity_ref[0, :, lanes])
        entering = spread_out(shell_of(lanes), speeds, spread_ref[...])
        flow = own_flow(value, speeds, derivative_ref[...]) + entering
        first = value + TIME_STEP * (flow + change_ref[0, 0, :, lanes])
        first_ref[0, 0, :, lanes] = first
        again = own_flow(first, speeds, derivative_ref[...])
        rest_ref[0, 0, :, lanes] = 0.5 * value + 0.5 * (first + TIME_STEP * again)


def stage(order, value, flux, change, jacobian, velocities, derivative, spread):
    chunks, elements, nodes, width = value.shape
    rows = flux.shape[1]
    block = pl.BlockSpec((1, 1, nodes, width), lambda c, e, order_ref: (order_ref[c], e, 0, 0))
    fixed = [
        pl.BlockSpec(part.shape, lambda c, e, order_ref: (0, 0)) for part in (derivative, spread)
    ]
    return pl.pallas_call(
        stage_kernel,
        grid_spec=pltpu.PrefetchScalarGridSpec(
            num_scalar_prefetch=1,
            grid=(chunks, elements),
            in_specs=[
                whole(pltpu.SMEM),
                pl.BlockSpec((1, 3, width), lambda c, e, order_ref: (order_ref[c], 0, 0)),
                *fixed,
                block,
                pl.BlockSpec((1, rows, width), lambda c, e, order_ref: (c, 0, 0)),
                block,
            ],
            out_specs=[block, block],
            scratch_shapes=[pltpu.VMEM((SHELL_ROWS - SHELL_MAIN, width), jnp.float32)],
        ),
        out_shape=[jax.ShapeDtypeStruct(value.shape, jnp.float32)] * 2,
        compiler_params=params(16),
        cost_estimate=cost(2 * 450 * 192 * value.size // 64, 4 * (4 * value.size + flux.size)),
        name="stage",
    )(order, jacobian, velocities, derivative, spread, value, flux, change)


def collide_kernel(slots, scale, column_ref, *refs):
    piece_refs = refs[:slots]
    weight_ref, density_ref = refs[slots : slots + 2]
    out_ref = refs[slots + 2 + (scale is not None)]
    pieces = [ref[0] for ref in piece_refs]
    high, low = halves(jnp.concatenate(pieces, 1))
    weight_high, weight_low = halves(
        jnp.concatenate([weight_ref[0, slot] for slot in range(slots)], 1)
    )

    def times(left, right):
        return lax.dot_general(
            left, right, (((1,), (1,)), ((), ())), preferred_element_type=jnp.float32
        )

    applied = times(high, weight_high) + (times(high, weight_low) + times(low, weight_high))
    change = density_ref[...] * (applied - pieces[0])
    if scale is None:
        out_ref[0] = change
        at = 0
        for start in range(0, out_ref.shape[1], SIDE**3):
            for a, b in surface_runs():
                refs[-1][0, at : at + b - a, :] = out_ref[0, start + a : start + b, :]
                at += b - a
    else:
        out_ref[0] = refs[slots + 2][0] + scale * change


def collide(value, weights, columns, density, rest=None, scale=None):
    _, rows, width = value.shape
    blocks, slots, span, _ = weights.shape
    per = width // span

    def piece(slot):
        def index(b, column_ref):
            column = column_ref[b * slots + slot]
            return (column // per, 0, column % per)

        return pl.BlockSpec((1, rows, span), index)

    def result(count):
        return pl.BlockSpec((1, count, span), lambda b, column_ref: (b // per, 0, b % per))

    out_specs, out_shape = result(rows), jax.ShapeDtypeStruct(value.shape, jnp.float32)
    if rest is None:
        seen = rows // SIDE**3 * len(surface_nodes())
        out_specs = [out_specs, result(seen)]
        out_shape = [out_shape, jax.ShapeDtypeStruct((value.shape[0], seen, width), jnp.float32)]
    in_specs = [piece(slot) for slot in range(slots)]
    in_specs.append(pl.BlockSpec((1, slots, span, span), lambda b, column_ref: (b, 0, 0, 0)))
    in_specs.append(pl.BlockSpec((rows, span), lambda b, column_ref: (0, 0)))
    operands = [value] * slots + [weights, density]
    if rest is not None:
        in_specs.append(out_specs)
        operands.append(rest)
    return pl.pallas_call(
        functools.partial(collide_kernel, slots, scale),
        grid_spec=pltpu.PrefetchScalarGridSpec(
            num_scalar_prefetch=1, grid=(blocks,), in_specs=in_specs, out_specs=out_specs
        ),
        out_shape=out_shape,
        compiler_params=params(24),
        cost_estimate=cost(
            12 * rows * blocks * slots * span * span,
            4 * (value.size * (slots + 1 + (rest is not None)) + weights.size),
        ),
        name="collide",
    )(columns, *operands)


def surface_runs():
    runs = []
    for node in range(SIDE**3):
        index = (node // 16, node // 4 % 4, node % 4)
        if any(i in (0, SIDE - 1) for i in index):
            if runs and runs[-1][1] == node:
                runs[-1][1] = node + 1
            else:
                runs.append([node, node + 1])
    return runs


def surface_nodes():
    return [node for a, b in surface_runs() for node in range(a, b)]


def after(value, other):
    return lax.optimization_barrier((value, other))[0]


def body(
    n_space,
    n_vel,
    distribution,
    inverse_jacobian,
    density,
    collision_blocks,
    block_columns,
    send_lists,
    exterior_faces,
):
    elements, nodes, width = distribution.shape
    owned = elements // n_vel
    rows = owned * nodes
    cap = send_lists.shape[2]
    local_faces = FACES * elements
    space_id = lax.axis_index("space")
    vel_id = lax.axis_index("vel")
    paired = n_space & (n_space - 1) == 0

    def partner(rank, step):
        return rank ^ step if paired else (rank + step) % n_space

    vel_paired = n_vel & (n_vel - 1) == 0

    def to_peer(rank, step):
        return rank ^ step if vel_paired else (rank + step) % n_vel

    def from_peer(rank, step):
        return rank ^ step if vel_paired else (rank - step) % n_vel

    def hand_over(value):
        blocks = [
            lax.dynamic_index_in_dim(value, to_peer(vel_id, step), 0, False) for step in range(n_vel)
        ]
        blocks = list(lax.optimization_barrier(blocks))
        for step in range(1, n_vel):
            pairs = [(i, to_peer(i, step)) for i in range(n_vel)]
            blocks[step] = lax.ppermute(blocks[step], "vel", pairs)
        return blocks

    steps = range(1, n_space)
    send_rows = send_lists[0]
    send_ids = jnp.concatenate(
        [lax.dynamic_index_in_dim(send_rows, partner(space_id, step), 0, False) for step in steps]
    )
    lookup = exterior_faces.reshape(-1)
    source = (lookup - local_faces) // cap
    slot = (lookup - local_faces) % cap
    back = source ^ space_id if paired else (space_id - source) % n_space
    received = jnp.where(back == 0, 0, local_faces + (back - 1) * cap + slot)
    lookup = jnp.where(
        lookup < local_faces,
        lookup,
        jnp.where(
            lookup >= local_faces + n_space * cap, local_faces + (n_space - 1) * cap, received
        ),
    )

    jacobian = inverse_jacobian.reshape(-1)
    own_jacobian = lax.dynamic_slice_in_dim(jacobian, vel_id * owned * 9, owned * 9)
    own_density = lax.dynamic_slice_in_dim(density, vel_id * owned, owned).reshape(rows, 1)
    own_density = jnp.broadcast_to(own_density, (rows, collision_blocks.shape[2]))
    velocities = grid_velocities(0, n_vel * width).reshape(3, n_vel, width).transpose(1, 0, 2)
    velocity = grid_velocities(vel_id * width, width)
    columns = block_columns.reshape(-1)
    derivative = jnp.asarray(derivative_parts())
    lift = jnp.asarray(lift_parts())
    pack = jnp.asarray(pack_parts())
    spread = jnp.asarray(spread_parts())

    def exchange(value):
        return lax.all_to_all(value, "vel", split_axis=0, concat_axis=0, tiled=True)

    def neighbours(values, matrix, scale):
        table, *outgoing = faces(values, send_ids, n_space - 1, cap)
        incoming = jnp.concatenate(
            [
                lax.ppermute(out, "space", [(i, partner(i, step)) for i in range(n_space)])
                for step, out in zip(steps, outgoing)
            ]
        )
        return inflow(table, incoming, lookup, jacobian, velocity, matrix, scale, n_vel)

    value_own = exchange(distribution.reshape(n_vel, rows, width))
    flux = neighbours([distribution], pack, None)
    start = guess(distribution, flux, jacobian, velocity, derivative, spread)

    flux, start = lax.optimization_barrier((flux, start))
    flux_own = hand_over(flux)
    value_own = after(value_own, start)
    change, seen = collide(value_own, collision_blocks, columns, own_density)

    seen = exchange(seen)
    flux_own = jnp.stack(flux_own)
    shape = (n_vel, owned, nodes, width)
    first, rest = stage(
        jnp.stack([from_peer(vel_id, step) for step in range(n_vel)]),
        value_own.reshape(shape),
        flux_own,
        change.reshape(shape),
        own_jacobian,
        velocities,
        derivative,
        spread,
    )
    total = collide(
        first.reshape(n_vel, rows, width),
        collision_blocks,
        columns,
        own_density,
        rest.reshape(n_vel, rows, width),
        0.5 * TIME_STEP,
    )

    totals = hand_over(total)
    seen = after(seen, total)
    seen = seen.reshape(elements, -1, width)
    outer = neighbours([start, seen], lift, 0.5 * TIME_STEP)
    result = outer.reshape(n_vel, rows, width)
    for step, block in enumerate(totals):
        at = from_peer(vel_id, step)
        block = block + lax.dynamic_index_in_dim(result, at, 0, False)
        result = lax.dynamic_update_index_in_dim(result, block, at, 0)
    return result.reshape(distribution.shape)


def solution(mesh):
    in_specs = (
        P("space", None, "vel"),
        P("space", None, None),
        P("space", None),
        P(),
        P(),
        P("space", None, None),
        P("space", None),
    )
    out_specs = P("space", None, "vel")

    def step(*arguments):
        return body(mesh.shape["space"], mesh.shape["vel"], *arguments)

    return jax.shard_map(
        step, mesh=mesh, in_specs=in_specs, out_specs=out_specs, check_vma=False
    )
```

profile of v0, /device:TPU:21, one launch (start us, length us, event | category | flops | bytes accessed | tf_op | source)
XLA Modules:
  0.0 881.1 jit_solution(2962166087797118392)
XLA Ops:
  0.0 5.6 all-to-all-start
  5.8 12.8 %faces.2 = (f32[384,16,512]{2,1,0:T(8,128)}, f32[48,16,512]{2,1,0:T(8,128)}, f32[48,16,512]{2,1,0:T(8,128)}, f32[48,16,512]{2,1,0:T(8,128)S(1)}) custom-call(s32[144]{0:T(256)S(1)} %pad_add_fusion.send_ref, f32[64,64,512]{2,1,0:T(8,128)} %value_ref.1), custom_call_target="tpu_custom_call" | custom-call | bytes 51380224 | tf_op jit(solution)/shard_map/faces/pallas_call | solution.py:258
  22.3 32.2 %collective-permute-done = f32[48,16,512]{2,1,0:T(8,128)S(1)} collective-permute-done((f32[48,16,512]{2,1,0:T(8,128)}, f32[48,16,512]{2,1,0:T(8,128)S(1)}, u32[]{:S(2)}, u32[]{:S(2)}) %collective-permute-start) | collective-permute-done | bytes 1572896 | tf_op jit(solution)/shard_map/ppermute | solution.py:585
  54.5 34.6 %collective-permute-done.1 = f32[48,16,512]{2,1,0:T(8,128)} collective-permute-done((f32[48,16,512]{2,1,0:T(8,128)}, f32[48,16,512]{2,1,0:T(8,128)}, u32[]{:S(2)}, u32[]{:S(2)}) %collective-permute-start.1) | collective-permute-done | bytes 1572896 | tf_op jit(solution)/shard_map/ppermute | solution.py:585
  92.2 21.4 %inflow.2.flux_ref = f32[8,296,512]{2,1,0:T(8,128)S(1)} custom-call(s32[384]{0:T(512)S(1)} %compare_select_fusion.2.lookup_ref, f32[576]{0:T(1024)S(1)} %reshape.435.jacobian_ref, f32[3,512]{1,0:T(4,128)S(1)} %pad_maximum_fusion.2.velocity_ref, bf16[40,384]{1,0:T(8,128)(2,1)S(1)} %copy-done.12, f32[384,16,512]{2,1,0:T(8,128)} %get-tuple-element.37.table_ref, ...), custom_call_target="tpu_custom_call" | custom-call | bytes 44302336 | tf_op jit(solution)/shard_map/inflow/pallas_call | solution.py:313
  113.6 23.5 %guess.1.refs_0_ = f32[64,64,512]{2,1,0:T(8,128)S(1)} custom-call(f32[576]{0:T(1024)S(1)} %reshape.435.jacobian_ref, f32[3,512]{1,0:T(4,128)S(1)} %pad_maximum_fusion.2.velocity_ref, bf16[192,192]{1,0:T(8,128)(2,1)S(1)} %copy-done.9, bf16[64,640]{1,0:T(8,128)(2,1)S(1)} %copy-done.10, f32[64,64,512]{2,1,0:T(8,128)S(1)} %bitcast.128, ...), custom_call_target="tpu_custom_call" | custom-call | flops 3221225472 | bytes 21626880 | tf_op jit(solution)/shard_map/guess/pallas_call | solution.py:341
  139.4 3.4 copy-done.3
  142.8 42.9 %all-to-all-done.refs_0_.refs_1_.refs_2_.refs_3_.refs_4_.refs_5_ = f32[8,512,512]{2,1,0:T(8,128)} async-done(((f32[8,512,512]{2,1,0:T(8,128)}), f32[8,512,512]{2,1,0:T(8,128)}, u32[]{:S(2)}, u32[]{:S(2)}) %all-to-all-start) | async-done | bytes 8388640 | tf_op jit(solution)/shard_map/all_to_all | solution.py:579
  185.8 42.8 %collide.2 = (f32[8,512,512]{2,1,0:T(8,128)S(1)}, f32[8,448,512]{2,1,0:T(8,128)S(1)}) custom-call(s32[192]{0:T(256)S(1)} %reshape.436.column_ref, f32[8,512,512]{2,1,0:T(8,128)} %all-to-all-done.refs_0_.refs_1_.refs_2_.refs_3_.refs_4_.refs_5_, f32[8,512,512]{2,1,0:T(8,128)} %all-to-all-done.refs_0_.refs_1_.refs_2_.refs_3_.refs_4_.refs_5_, ...), custom_call_target="tpu_custom_call" | custom-call | flops 19327352832 | bytes 71303168 | tf_op jit(solution)/shard_map/collide/pallas_call | solution.py:472
  228.6 3.3 copy-done.6
  234.9 8.7 all-to-all-start.1
  243.6 4.0 dynamic-slice_bitcast_fusion.8
  255.7 121.2 %collective-permute-done.4 = f32[296,512]{1,0:T(8,128)S(1)} collective-permute-done((f32[296,512]{1,0:T(8,128)}, f32[296,512]{1,0:T(8,128)S(1)}, u32[]{:S(2)}, u32[]{:S(2)}) %collective-permute-start.4) | collective-permute-done | bytes 606240 | tf_op jit(solution)/shard_map/ppermute | solution.py:545
  377.0 13.8 %collective-permute-done.5 = f32[296,512]{1,0:T(8,128)S(1)} collective-permute-done((f32[296,512]{1,0:T(8,128)}, f32[296,512]{1,0:T(8,128)S(1)}, u32[]{:S(2)}, u32[]{:S(2)}) %collective-permute-start.5) | collective-permute-done | bytes 606240 | tf_op jit(solution)/shard_map/ppermute | solution.py:545
  390.9 75.1 %collective-permute-done.6 = f32[296,512]{1,0:T(8,128)S(1)} collective-permute-done((f32[296,512]{1,0:T(8,128)S(1)}, f32[296,512]{1,0:T(8,128)S(1)}, u32[]{:S(2)}, u32[]{:S(2)}) %collective-permute-start.6) | collective-permute-done | bytes 606240 | tf_op jit(solution)/shard_map/ppermute | solution.py:545
  466.1 12.9 %collective-permute-done.7 = f32[296,512]{1,0:T(8,128)S(1)} collective-permute-done((f32[296,512]{1,0:T(8,128)S(1)}, f32[296,512]{1,0:T(8,128)S(1)}, u32[]{:S(2)}, u32[]{:S(2)}) %collective-permute-start.7) | collective-permute-done | bytes 606240 | tf_op jit(solution)/shard_map/ppermute | solution.py:545
  479.0 14.3 %collective-permute-done.8 = f32[296,512]{1,0:T(8,128)S(1)} collective-permute-done((f32[296,512]{1,0:T(8,128)S(1)}, f32[296,512]{1,0:T(8,128)S(1)}, u32[]{:S(2)}, u32[]{:S(2)}) %collective-permute-start.8) | collective-permute-done | bytes 606240 | tf_op jit(solution)/shard_map/ppermute | solution.py:545
  493.4 12.9 %collective-permute-done.9 = f32[296,512]{1,0:T(8,128)S(1)} collective-permute-done((f32[296,512]{1,0:T(8,128)S(1)}, f32[296,512]{1,0:T(8,128)S(1)}, u32[]{:S(2)}, u32[]{:S(2)}) %collective-permute-start.9) | collective-permute-done | bytes 606240 | tf_op jit(solution)/shard_map/ppermute | solution.py:545
  506.4 3.4 copy-done.7
  509.7 56.2 %stage.1 = (f32[8,8,64,512]{3,2,1,0:T(8,128)S(1)}, f32[8,8,64,512]{3,2,1,0:T(8,128)S(1)}) custom-call(s32[8]{0:T(128)S(1)} %stack.75.order_ref, f32[72]{0:T(128)S(1)} %dynamic_slice.94.jacobian_ref, f32[8,3,512]{2,1,0:T(4,128)S(1)} %maximum_bitcast_fusion.velocity_ref, bf16[192,192]{1,0:T(8,128)(2,1)S(1)} %copy-done.9, bf16[64,640]{1,0:T(8,128)(2,1)S(1)} %copy-done.10, ...), custom_call_target="tpu_custom_call" | custom-call | flops 5662310400 | bytes 38404096 | tf_op jit(solution)/shard_map/stage/pallas_call | solution.py:394
  566.0 42.2 %collide.3 = f32[8,512,512]{2,1,0:T(8,128)S(1)} custom-call(s32[192]{0:T(256)S(1)} %reshape.436.column_ref, f32[8,512,512]{2,1,0:T(8,128)S(1)} %bitcast.120, f32[8,512,512]{2,1,0:T(8,128)S(1)} %bitcast.121, f32[8,512,512]{2,1,0:T(8,128)S(1)} %bitcast.122, f32[8,512,512]{2,1,0:T(8,128)S(1)} %bitcast.123, f32[8,512,512]{2,1,0:T(8,128)S(1)} %bitcast.124, ...), custom_call_target="tpu_custom_call" | custom-call | flops 19327352832 | bytes 79691776 | tf_op jit(solution)/shard_map/collide/pallas_call | solution.py:472
  608.2 3.3 copy-done.4
  611.5 15.9 %faces.3 = (f32[384,16,512]{2,1,0:T(8,128)}, f32[48,16,512]{2,1,0:T(8,128)S(1)}, f32[48,16,512]{2,1,0:T(8,128)S(1)}, f32[48,16,512]{2,1,0:T(8,128)S(1)}) custom-call(s32[144]{0:T(256)S(1)} %pad_add_fusion.send_ref, f32[64,64,512]{2,1,0:T(8,128)} %copy-done.3, f32[64,56,512]{2,1,0:T(8,128)} %bitcast.33.refs_1_), custom_call_target="tpu_custom_call" | custom-call | bytes 66060288 | tf_op jit(solution)/shard_map/faces/pallas_call | solution.py:258
  634.3 28.6 %collective-permute-done.10 = f32[48,16,512]{2,1,0:T(8,128)S(1)} collective-permute-done((f32[48,16,512]{2,1,0:T(8,128)S(1)}, f32[48,16,512]{2,1,0:T(8,128)S(1)}, u32[]{:S(2)}, u32[]{:S(2)}) %collective-permute-start.10) | collective-permute-done | bytes 1572896 | tf_op jit(solution)/shard_map/ppermute | solution.py:585
  662.9 34.6 %collective-permute-done.11 = f32[48,16,512]{2,1,0:T(8,128)S(1)} collective-permute-done((f32[48,16,512]{2,1,0:T(8,128)S(1)}, f32[48,16,512]{2,1,0:T(8,128)S(1)}, u32[]{:S(2)}, u32[]{:S(2)}) %collective-permute-start.11) | collective-permute-done | bytes 1572896 | tf_op jit(solution)/shard_map/ppermute | solution.py:585
  697.5 4.1 collective-permute-start.17
  702.3 4.6 copy-done.5
  706.8 17.5 %inflow.3 = f32[64,64,512]{2,1,0:T(8,128)} custom-call(s32[384]{0:T(512)S(1)} %compare_select_fusion.2.lookup_ref, f32[576]{0:T(1024)S(1)} %reshape.435.jacobian_ref, f32[3,512]{1,0:T(4,128)S(1)} %pad_maximum_fusion.2.velocity_ref, bf16[64,192]{1,0:T(8,128)(2,1)S(1)} %copy-done.11, f32[384,16,512]{2,1,0:T(8,128)S(1)} %copy-done.5, ...), custom_call_target="tpu_custom_call" | custom-call | bytes 51380224 | tf_op jit(solution)/shard_map/inflow/pallas_call | solution.py:313
  739.3 69.6 %collective-permute-done.16 = f32[512,512]{1,0:T(8,128)S(1)} collective-permute-done((f32[512,512]{1,0:T(8,128)}, f32[512,512]{1,0:T(8,128)S(1)}, u32[]{:S(2)}, u32[]{:S(2)}) %collective-permute-start.16) | collective-permute-done | bytes 1048608 | tf_op jit(solution)/shard_map/ppermute | solution.py:545
  811.4 19.9 %collective-permute-done.17 = f32[512,512]{1,0:T(8,128)S(1)} collective-permute-done((f32[512,512]{1,0:T(8,128)S(1)}, f32[512,512]{1,0:T(8,128)S(1)}, u32[]{:S(2)}, u32[]{:S(2)}) %collective-permute-start.17) | collective-permute-done | bytes 1048608 | tf_op jit(solution)/shard_map/ppermute | solution.py:545
  833.8 23.0 %collective-permute-done.18 = f32[512,512]{1,0:T(8,128)S(1)} collective-permute-done((f32[512,512]{1,0:T(8,128)S(1)}, f32[512,512]{1,0:T(8,128)S(1)}, u32[]{:S(2)}, u32[]{:S(2)}) %collective-permute-start.18) | collective-permute-done | bytes 1048608 | tf_op jit(solution)/shard_map/ppermute | solution.py:545
  859.2 20.7 %collective-permute-done.19 = f32[512,512]{1,0:T(8,128)S(1)} collective-permute-done((f32[512,512]{1,0:T(8,128)S(1)}, f32[512,512]{1,0:T(8,128)S(1)}, u32[]{:S(2)}, u32[]{:S(2)}) %collective-permute-start.19) | collective-permute-done | bytes 1048608 | tf_op jit(solution)/shard_map/ppermute | solution.py:545
  (115 shorter events, 51.6 us)
Async XLA Ops:
  0.0 21.2 %copy-start = (f32[64,64]{1,0:T(8,128)S(1)}, f32[64,64]{1,0:T(8,128)}, u32[]{:S(2)}) copy-start(f32[64,64]{1,0:T(8,128)} %param.13) | copy-start | bytes 49156
  0.0 185.7 %all-to-all-start = ((f32[8,512,512]{2,1,0:T(8,128)}), f32[8,512,512]{2,1,0:T(8,128)}, u32[]{:S(2)}, u32[]{:S(2)}) async-start(f32[8,512,512]{2,1,0:T(8,128)} %bitcast.126), calls=%async_computation | async-start | bytes 16777216 | tf_op jit(solution)/shard_map/all_to_all | solution.py:579
  18.6 35.9 %collective-permute-start = (f32[48,16,512]{2,1,0:T(8,128)}, f32[48,16,512]{2,1,0:T(8,128)S(1)}, u32[]{:S(2)}, u32[]{:S(2)}) collective-permute-start(f32[48,16,512]{2,1,0:T(8,128)} %get-tuple-element.38), channel_id=1, source_target_pairs={{0,8},{8,0},{16,24},{24,16},{1,9},{9,1},{17,25},{25,17},{2,10},{10... | collective-permute-start | bytes 4718600 | tf_op jit(solution)/shard_map/ppermute | solution.py:585
  19.8 69.3 %collective-permute-start.1 = (f32[48,16,512]{2,1,0:T(8,128)}, f32[48,16,512]{2,1,0:T(8,128)}, u32[]{:S(2)}, u32[]{:S(2)}) collective-permute-start(f32[48,16,512]{2,1,0:T(8,128)} %get-tuple-element.39), channel_id=1, source_target_pairs={{0,16},{8,24},{16,0},{24,8},{1,17},{9,25},{17,1},{25,9},{2,18},{10... | collective-permute-start | bytes 4718600 | tf_op jit(solution)/shard_map/ppermute | solution.py:585
  20.0 69.1 %collective-permute-start.2 = (f32[48,16,512]{2,1,0:T(8,128)S(1)}, f32[48,16,512]{2,1,0:T(8,128)}, u32[]{:S(2)}, u32[]{:S(2)}) collective-permute-start(f32[48,16,512]{2,1,0:T(8,128)S(1)} %get-tuple-element.40), channel_id=1, source_target_pairs={{0,24},{8,16},{16,8},{24,0},{1,25},{9,17},{17,9},{25,1},{2,26},{10... | collective-permute-start | bytes 4718600 | tf_op jit(solution)/shard_map/ppermute | solution.py:585
  21.8 70.3 %copy-start.12 = (bf16[40,384]{1,0:T(8,128)(2,1)S(1)}, bf16[40,384]{1,0:T(8,128)(2,1)}, u32[]{:S(2)}) copy-start(bf16[40,384]{1,0:T(8,128)(2,1)} %constant.251.clone.lift_ref) | copy-start | bytes 92164
  89.1 24.4 %slice-start = ((s8[8388608]{0:T(1024)(128)(4,1)}), s8[4194304]{0:T(1024)(128)(4,1)S(1)}, s32[]{:S(2)}) async-start(s8[8388608]{0:T(1024)(128)(4,1)} %bitcast.127), calls=%async_computation.2 | async-start | bytes 8388608
  92.1 21.4 %slice-start.1 = ((s8[8388608]{0:T(1024)(128)(4,1)}), s8[4194304]{0:T(1024)(128)(4,1)S(1)}, s32[]{:S(2)}) async-start(s8[8388608]{0:T(1024)(128)(4,1)} %bitcast.127), calls=%async_computation.3 | async-start | bytes 8388608
  92.1 21.4 %copy-start.9 = (bf16[192,192]{1,0:T(8,128)(2,1)S(1)}, bf16[192,192]{1,0:T(8,128)(2,1)}, u32[]{:S(2)}) copy-start(bf16[192,192]{1,0:T(8,128)(2,1)} %constant.249.clone.derivative_ref) | copy-start | bytes 221188
  92.1 21.4 %copy-start.10 = (bf16[64,640]{1,0:T(8,128)(2,1)S(1)}, bf16[64,640]{1,0:T(8,128)(2,1)}, u32[]{:S(2)}) copy-start(bf16[64,640]{1,0:T(8,128)(2,1)} %constant.252.clone.spread_ref) | copy-start | bytes 245764
  234.9 376.6 %all-to-all-start.1 = ((f32[8,448,512]{2,1,0:T(8,128)}), f32[8,448,512]{2,1,0:T(8,128)}, u32[]{:S(2)}, u32[]{:S(2)}) async-start(f32[8,448,512]{2,1,0:T(8,128)} %copy-done.8), calls=%async_computation.1 | async-start | bytes 14680064 | tf_op jit(solution)/shard_map/all_to_all | solution.py:579
  247.7 6.6 collective-permute-start.3
  249.0 127.9 %collective-permute-start.4 = (f32[296,512]{1,0:T(8,128)}, f32[296,512]{1,0:T(8,128)S(1)}, u32[]{:S(2)}, u32[]{:S(2)}) collective-permute-start(f32[296,512]{1,0:T(8,128)} %get-tuple-element.47), channel_id=1, source_target_pairs={{0,2},{1,3},{2,0},{3,1},{4,6},{5,7},{6,4},{7,5},{8,10},{9,11},{10,... | collective-permute-start | bytes 1818632 | tf_op jit(solution)/shard_map/ppermute | solution.py:545
  250.9 139.9 %collective-permute-start.5 = (f32[296,512]{1,0:T(8,128)}, f32[296,512]{1,0:T(8,128)S(1)}, u32[]{:S(2)}, u32[]{:S(2)}) collective-permute-start(f32[296,512]{1,0:T(8,128)} %get-tuple-element.48), channel_id=1, source_target_pairs={{0,3},{1,2},{2,1},{3,0},{4,7},{5,6},{6,5},{7,4},{8,11},{9,10},{10,... | collective-permute-start | bytes 1818632 | tf_op jit(solution)/shard_map/ppermute | solution.py:545
  251.6 214.5 %collective-permute-start.6 = (f32[296,512]{1,0:T(8,128)S(1)}, f32[296,512]{1,0:T(8,128)S(1)}, u32[]{:S(2)}, u32[]{:S(2)}) collective-permute-start(f32[296,512]{1,0:T(8,128)S(1)} %get-tuple-element.49), channel_id=1, source_target_pairs={{0,4},{1,5},{2,6},{3,7},{4,0},{5,1},{6,2},{7,3},{8,12},{9,13},{10,... | collective-permute-start | bytes 1818632 | tf_op jit(solution)/shard_map/ppermute | solution.py:545
  251.6 227.4 %collective-permute-start.7 = (f32[296,512]{1,0:T(8,128)S(1)}, f32[296,512]{1,0:T(8,128)S(1)}, u32[]{:S(2)}, u32[]{:S(2)}) collective-permute-start(f32[296,512]{1,0:T(8,128)S(1)} %get-tuple-element.50), channel_id=1, source_target_pairs={{0,5},{1,4},{2,7},{3,6},{4,1},{5,0},{6,3},{7,2},{8,13},{9,12},{10,... | collective-permute-start | bytes 1818632 | tf_op jit(solution)/shard_map/ppermute | solution.py:545
  254.2 239.1 %collective-permute-start.8 = (f32[296,512]{1,0:T(8,128)S(1)}, f32[296,512]{1,0:T(8,128)S(1)}, u32[]{:S(2)}, u32[]{:S(2)}) collective-permute-start(f32[296,512]{1,0:T(8,128)S(1)} %get-tuple-element.51), channel_id=1, source_target_pairs={{0,6},{1,7},{2,4},{3,5},{4,2},{5,3},{6,0},{7,1},{8,14},{9,15},{10,... | collective-permute-start | bytes 1818632 | tf_op jit(solution)/shard_map/ppermute | solution.py:545
  376.8 129.5 %collective-permute-start.9 = (f32[296,512]{1,0:T(8,128)S(1)}, f32[296,512]{1,0:T(8,128)S(1)}, u32[]{:S(2)}, u32[]{:S(2)}) collective-permute-start(f32[296,512]{1,0:T(8,128)S(1)} %get-tuple-element.52), channel_id=1, source_target_pairs={{0,7},{1,6},{2,5},{3,4},{4,3},{5,2},{6,1},{7,0},{8,15},{9,14},{10,... | collective-permute-start | bytes 1818632 | tf_op jit(solution)/shard_map/ppermute | solution.py:545
  611.5 18.5 %slice-start.2 = ((s8[8388608]{0:T(1024)(128)(4,1)}), s8[4194304]{0:T(1024)(128)(4,1)S(1)}, s32[]{:S(2)}) async-start(s8[8388608]{0:T(1024)(128)(4,1)} %bitcast.129), calls=%async_computation.4 | async-start | bytes 8388608
  611.5 18.5 %slice-start.3 = ((s8[8388608]{0:T(1024)(128)(4,1)}), s8[4194304]{0:T(1024)(128)(4,1)S(1)}, s32[]{:S(2)}) async-start(s8[8388608]{0:T(1024)(128)(4,1)} %bitcast.129), calls=%async_computation.5 | async-start | bytes 8388608
  627.4 35.6 %collective-permute-start.10 = (f32[48,16,512]{2,1,0:T(8,128)S(1)}, f32[48,16,512]{2,1,0:T(8,128)S(1)}, u32[]{:S(2)}, u32[]{:S(2)}) collective-permute-start(f32[48,16,512]{2,1,0:T(8,128)S(1)} %get-tuple-element.58), channel_id=1, source_target_pairs={{0,8},{8,0},{16,24},{24,16},{1,9},{9,1},{17,25},{25,17},{2,10},{10... | collective-permute-start | bytes 4718600 | tf_op jit(solution)/shard_map/ppermute | solution.py:585
  628.6 68.9 %collective-permute-start.11 = (f32[48,16,512]{2,1,0:T(8,128)S(1)}, f32[48,16,512]{2,1,0:T(8,128)S(1)}, u32[]{:S(2)}, u32[]{:S(2)}) collective-permute-start(f32[48,16,512]{2,1,0:T(8,128)S(1)} %get-tuple-element.59), channel_id=1, source_target_pairs={{0,16},{8,24},{16,0},{24,8},{1,17},{9,25},{17,1},{25,9},{2,18},{10... | collective-permute-start | bytes 4718600 | tf_op jit(solution)/shard_map/ppermute | solution.py:585
  628.8 68.7 %collective-permute-start.12 = (f32[48,16,512]{2,1,0:T(8,128)S(1)}, f32[48,16,512]{2,1,0:T(8,128)S(1)}, u32[]{:S(2)}, u32[]{:S(2)}) collective-permute-start(f32[48,16,512]{2,1,0:T(8,128)S(1)} %get-tuple-element.60), channel_id=1, source_target_pairs={{0,24},{8,16},{16,8},{24,0},{1,25},{9,17},{17,9},{25,1},{2,26},{10... | collective-permute-start | bytes 4718600 | tf_op jit(solution)/shard_map/ppermute | solution.py:585
  633.0 69.2 %copy-start.11 = (bf16[64,192]{1,0:T(8,128)(2,1)S(1)}, bf16[64,192]{1,0:T(8,128)(2,1)}, u32[]{:S(2)}) copy-start(bf16[64,192]{1,0:T(8,128)(2,1)} %constant.250.clone.lift_ref) | copy-start | bytes 73732
  633.0 95.0 %collective-permute-start.13 = (f32[512,512]{1,0:T(8,128)}, f32[512,512]{1,0:T(8,128)}, u32[]{:S(2)}, u32[]{:S(2)}) collective-permute-start(f32[512,512]{1,0:T(8,128)} %get-tuple-element.62), channel_id=1, source_target_pairs={{0,1},{1,0},{2,3},{3,2},{4,5},{5,4},{6,7},{7,6},{8,9},{9,8},{10,11... | collective-permute-start | bytes 3145736 | tf_op jit(solution)/shard_map/ppermute | solution.py:545
  634.3 98.8 %collective-permute-start.14 = (f32[512,512]{1,0:T(8,128)}, f32[512,512]{1,0:T(8,128)}, u32[]{:S(2)}, u32[]{:S(2)}) collective-permute-start(f32[512,512]{1,0:T(8,128)} %get-tuple-element.63), channel_id=1, source_target_pairs={{0,2},{1,3},{2,0},{3,1},{4,6},{5,7},{6,4},{7,5},{8,10},{9,11},{10,... | collective-permute-start | bytes 3145736 | tf_op jit(solution)/shard_map/ppermute | solution.py:545
  662.9 73.9 %collective-permute-start.15 = (f32[512,512]{1,0:T(8,128)}, f32[512,512]{1,0:T(8,128)S(1)}, u32[]{:S(2)}, u32[]{:S(2)}) collective-permute-start(f32[512,512]{1,0:T(8,128)} %get-tuple-element.64), channel_id=1, source_target_pairs={{0,3},{1,2},{2,1},{3,0},{4,7},{5,6},{6,5},{7,4},{8,11},{9,10},{10,... | collective-permute-start | bytes 3145736 | tf_op jit(solution)/shard_map/ppermute | solution.py:545
  697.5 111.4 %collective-permute-start.16 = (f32[512,512]{1,0:T(8,128)}, f32[512,512]{1,0:T(8,128)S(1)}, u32[]{:S(2)}, u32[]{:S(2)}) collective-permute-start(f32[512,512]{1,0:T(8,128)} %get-tuple-element.65), channel_id=1, source_target_pairs={{0,4},{1,5},{2,6},{3,7},{4,0},{5,1},{6,2},{7,3},{8,12},{9,13},{10,... | collective-permute-start | bytes 3145736 | tf_op jit(solution)/shard_map/ppermute | solution.py:545
  697.5 133.8 %collective-permute-start.17 = (f32[512,512]{1,0:T(8,128)S(1)}, f32[512,512]{1,0:T(8,128)S(1)}, u32[]{:S(2)}, u32[]{:S(2)}) collective-permute-start(f32[512,512]{1,0:T(8,128)S(1)} %get-tuple-element.66), channel_id=1, source_target_pairs={{0,5},{1,4},{2,7},{3,6},{4,1},{5,0},{6,3},{7,2},{8,13},{9,12},{10,... | collective-permute-start | bytes 3145736 | tf_op jit(solution)/shard_map/ppermute | solution.py:545
  728.1 128.7 %collective-permute-start.18 = (f32[512,512]{1,0:T(8,128)S(1)}, f32[512,512]{1,0:T(8,128)S(1)}, u32[]{:S(2)}, u32[]{:S(2)}) collective-permute-start(f32[512,512]{1,0:T(8,128)S(1)} %get-tuple-element.67), channel_id=1, source_target_pairs={{0,6},{1,7},{2,4},{3,5},{4,2},{5,3},{6,0},{7,1},{8,14},{9,15},{10,... | collective-permute-start | bytes 3145736 | tf_op jit(solution)/shard_map/ppermute | solution.py:545
  733.0 146.9 %collective-permute-start.19 = (f32[512,512]{1,0:T(8,128)S(1)}, f32[512,512]{1,0:T(8,128)S(1)}, u32[]{:S(2)}, u32[]{:S(2)}) collective-permute-start(f32[512,512]{1,0:T(8,128)S(1)} %get-tuple-element.68), channel_id=1, source_target_pairs={{0,7},{1,6},{2,5},{3,4},{4,3},{5,2},{6,1},{7,0},{8,15},{9,14},{10,... | collective-permute-start | bytes 3145736 | tf_op jit(solution)/shard_map/ppermute | solution.py:545
  831.3 49.8 %copy-start.1 = (f32[64,64]{1,0:T(8,128)S(1)}, f32[64,64]{1,0:T(8,128)}, u32[]{:S(2)}) copy-start(f32[64,64]{1,0:T(8,128)} %param.13) | copy-start | bytes 49156
  (11 other events, 76.6 us)
where the time goes:
time: 884 us; the launch traced here: 881 us
  waiting for transfers between devices  556 us (63%)
  Pallas kernels  232 us (26%)
  local copies, waits for them, and re-layouts  43.9 us (5%)
  starting transfers between devices  31.6 us (4%)
  other arithmetic  16.5 us (2%)
    ppermute x14, waiting for transfers between devices, hand_over(): blocks[step] = lax.ppermute(blocks[step], 'vel', pairs)  383 us
    ppermute x6, waiting for transfers between devices, neighbours(): lax.ppermute(out, 'space', [(i, partner(i, step)) for i in range(n_space)])  130 us
    pallas_call x2, Pallas kernels, collide(): pl.pallas_call(functools.partial(collide_kernel, slots, scale), grid_spec...  85 us
    pallas_call x1, Pallas kernels, stage(): pl.pallas_call(stage_kernel, grid_spec=pltpu.PrefetchScalarGridSpec(num_s...  56.2 us
    all_to_all x2, waiting for transfers between devices, exchange(): return lax.all_to_all(value, 'vel', split_axis=0, concat_axis=0, tiled=True)  42.9 us
    pallas_call x2, Pallas kernels, inflow(): pl.pallas_call(functools.partial(inflow_kernel, scale), out_shape=jax.Sha...  38.8 us
    pallas_call x2, Pallas kernels, faces(): pl.pallas_call(functools.partial(faces_kernel, cap, others), out_shape=ou...  28.7 us
    unnamed x52, local copies, waits for them, and re-layouts  24.9 us
  transfers between devices with their start and end apart: 22, of which 15 were waited for; matrix products, arithmetic and copies ran while one was open for 4% of the time, Pallas kernels for 20%

commit v1 on v0

--- a/solution.py
+++ b/solution.py
@@ -535,7 +535,7 @@
     def from_peer(rank, step):
         return rank ^ step if vel_paired else (rank - step) % n_vel
 
-    def hand_over(value):
+    def hand_over(value, wait_for_near=False):
         blocks = [
             lax.dynamic_index_in_dim(value, to_peer(vel_id, step), 0, False) for step in range(n_vel)
         ]
@@ -543,6 +543,8 @@
         for step in range(1, n_vel):
             pairs = [(i, to_peer(i, step)) for i in range(n_vel)]
             blocks[step] = lax.ppermute(blocks[step], "vel", pairs)
+            if step == 1 and wait_for_near:
+                blocks[2:] = lax.optimization_barrier(blocks[1:])[1:]
         return blocks
 
     steps = range(1, n_space)
@@ -593,7 +595,7 @@
     start = guess(distribution, flux, jacobian, velocity, derivative, spread)
 
     flux, start = lax.optimization_barrier((flux, start))
-    flux_own = hand_over(flux)
+    flux_own = hand_over(flux, True)
     value_own = after(value_own, start)
     change, seen = collide(value_own, collision_blocks, columns, own_density)
 

time: 884 us -> 884 us (level)
  transfers between devices with their start and end apart: 22 -> 22, of which waited for: 15 -> 16; matrix products, arithmetic and copies ran while one was open for 4% -> 4% of each run, Pallas kernels for 20% -> 20%
where the time goes in v1:
time: 884 us; the launch traced here: 881 us
  waiting for transfers between devices  556 us (63%)
  Pallas kernels  232 us (26%)
  local copies, waits for them, and re-layouts  43.9 us (5%)
  starting transfers between devices  31.6 us (4%)
  other arithmetic  16.5 us (2%)
    ppermute x14, waiting for transfers between devices, hand_over(): blocks[step] = lax.ppermute(blocks[step], 'vel', pairs)  383 us
    ppermute x6, waiting for transfers between devices, neighbours(): lax.ppermute(out, 'space', [(i, partner(i, step)) for i in range(n_space)])  130 us
    pallas_call x2, Pallas kernels, collide(): pl.pallas_call(functools.partial(collide_kernel, slots, scale), grid_spec...  85 us
    pallas_call x1, Pallas kernels, stage(): pl.pallas_call(stage_kernel, grid_spec=pltpu.PrefetchScalarGridSpec(num_s...  56.2 us
    all_to_all x2, waiting for transfers between devices, exchange(): return lax.all_to_all(value, 'vel', split_axis=0, concat_axis=0, tiled=True)  42.9 us
    pallas_call x2, Pallas kernels, inflow(): pl.pallas_call(functools.partial(inflow_kernel, scale), out_shape=jax.Sha...  38.8 us
    pallas_call x2, Pallas kernels, faces(): pl.pallas_call(functools.partial(faces_kernel, cap, others), out_shape=ou...  28.7 us
    unnamed x52, local copies, waits for them, and re-layouts  24.9 us
  transfers between devices with their start and end apart: 22, of which 16 were waited for; matrix products, arithmetic and copies ran while one was open for 4% of the time, Pallas kernels for 20%

profile of v1, /device:TPU:21, one launch (start us, length us, event | category | flops | bytes accessed | tf_op | source)
XLA Modules:
  0.0 881.1 jit_solution(12394104220907613094)
XLA Ops:
  0.0 5.6 all-to-all-start
  5.8 12.8 %faces.2 = (f32[384,16,512]{2,1,0:T(8,128)}, f32[48,16,512]{2,1,0:T(8,128)}, f32[48,16,512]{2,1,0:T(8,128)}, f32[48,16,512]{2,1,0:T(8,128)S(1)}) custom-call(s32[144]{0:T(256)S(1)} %pad_add_fusion.send_ref, f32[64,64,512]{2,1,0:T(8,128)} %value_ref.1), custom_call_target="tpu_custom_call" | custom-call | bytes 51380224 | tf_op jit(solution)/shard_map/faces/pallas_call | solution.py:258
  22.3 32.2 %collective-permute-done = f32[48,16,512]{2,1,0:T(8,128)S(1)} collective-permute-done((f32[48,16,512]{2,1,0:T(8,128)}, f32[48,16,512]{2,1,0:T(8,128)S(1)}, u32[]{:S(2)}, u32[]{:S(2)}) %collective-permute-start) | collective-permute-done | bytes 1572896 | tf_op jit(solution)/shard_map/ppermute | solution.py:587
  54.5 34.6 %collective-permute-done.1 = f32[48,16,512]{2,1,0:T(8,128)} collective-permute-done((f32[48,16,512]{2,1,0:T(8,128)}, f32[48,16,512]{2,1,0:T(8,128)}, u32[]{:S(2)}, u32[]{:S(2)}) %collective-permute-start.1) | collective-permute-done | bytes 1572896 | tf_op jit(solution)/shard_map/ppermute | solution.py:587
  92.2 21.4 %inflow.2.flux_ref = f32[8,296,512]{2,1,0:T(8,128)S(1)} custom-call(s32[384]{0:T(512)S(1)} %compare_select_fusion.2.lookup_ref, f32[576]{0:T(1024)S(1)} %reshape.435.jacobian_ref, f32[3,512]{1,0:T(4,128)S(1)} %pad_maximum_fusion.2.velocity_ref, bf16[40,384]{1,0:T(8,128)(2,1)S(1)} %copy-done.12, f32[384,16,512]{2,1,0:T(8,128)} %get-tuple-element.43.table_ref, ...), custom_call_target="tpu_custom_call" | custom-call | bytes 44302336 | tf_op jit(solution)/shard_map/inflow/pallas_call | solution.py:313
  113.6 23.5 %guess.1.refs_0_ = f32[64,64,512]{2,1,0:T(8,128)S(1)} custom-call(f32[576]{0:T(1024)S(1)} %reshape.435.jacobian_ref, f32[3,512]{1,0:T(4,128)S(1)} %pad_maximum_fusion.2.velocity_ref, bf16[192,192]{1,0:T(8,128)(2,1)S(1)} %copy-done.9, bf16[64,640]{1,0:T(8,128)(2,1)S(1)} %copy-done.10, f32[64,64,512]{2,1,0:T(8,128)S(1)} %bitcast.128, ...), custom_call_target="tpu_custom_call" | custom-call | flops 3221225472 | bytes 21626880 | tf_op jit(solution)/shard_map/guess/pallas_call | solution.py:341
  139.3 3.4 copy-done.3
  142.7 42.9 %all-to-all-done.refs_0_.refs_1_.refs_2_.refs_3_.refs_4_.refs_5_ = f32[8,512,512]{2,1,0:T(8,128)} async-done(((f32[8,512,512]{2,1,0:T(8,128)}), f32[8,512,512]{2,1,0:T(8,128)}, u32[]{:S(2)}, u32[]{:S(2)}) %all-to-all-start) | async-done | bytes 8388640 | tf_op jit(solution)/shard_map/all_to_all | solution.py:581
  185.8 42.8 %collide.2 = (f32[8,512,512]{2,1,0:T(8,128)S(1)}, f32[8,448,512]{2,1,0:T(8,128)S(1)}) custom-call(s32[192]{0:T(256)S(1)} %reshape.436.column_ref, f32[8,512,512]{2,1,0:T(8,128)} %all-to-all-done.refs_0_.refs_1_.refs_2_.refs_3_.refs_4_.refs_5_, f32[8,512,512]{2,1,0:T(8,128)} %all-to-all-done.refs_0_.refs_1_.refs_2_.refs_3_.refs_4_.refs_5_, ...), custom_call_target="tpu_custom_call" | custom-call | flops 19327352832 | bytes 71303168 | tf_op jit(solution)/shard_map/collide/pallas_call | solution.py:472
  228.6 3.3 copy-done.6
  234.9 8.7 all-to-all-start.1
  243.6 4.0 dynamic-slice_bitcast_fusion.8
  256.8 120.1 %collective-permute-done.4 = f32[296,512]{1,0:T(8,128)S(1)} collective-permute-done((f32[296,512]{1,0:T(8,128)}, f32[296,512]{1,0:T(8,128)S(1)}, u32[]{:S(2)}, u32[]{:S(2)}) %collective-permute-start.4) | collective-permute-done | bytes 606240 | tf_op jit(solution)/shard_map/ppermute | solution.py:545
  377.0 13.8 %collective-permute-done.5 = f32[296,512]{1,0:T(8,128)S(1)} collective-permute-done((f32[296,512]{1,0:T(8,128)}, f32[296,512]{1,0:T(8,128)S(1)}, u32[]{:S(2)}, u32[]{:S(2)}) %collective-permute-start.5) | collective-permute-done | bytes 606240 | tf_op jit(solution)/shard_map/ppermute | solution.py:545
  390.9 75.1 %collective-permute-done.6 = f32[296,512]{1,0:T(8,128)S(1)} collective-permute-done((f32[296,512]{1,0:T(8,128)S(1)}, f32[296,512]{1,0:T(8,128)S(1)}, u32[]{:S(2)}, u32[]{:S(2)}) %collective-permute-start.6) | collective-permute-done | bytes 606240 | tf_op jit(solution)/shard_map/ppermute | solution.py:545
  466.1 12.9 %collective-permute-done.7 = f32[296,512]{1,0:T(8,128)S(1)} collective-permute-done((f32[296,512]{1,0:T(8,128)S(1)}, f32[296,512]{1,0:T(8,128)S(1)}, u32[]{:S(2)}, u32[]{:S(2)}) %collective-permute-start.7) | collective-permute-done | bytes 606240 | tf_op jit(solution)/shard_map/ppermute | solution.py:545
  479.0 14.3 %collective-permute-done.8 = f32[296,512]{1,0:T(8,128)S(1)} collective-permute-done((f32[296,512]{1,0:T(8,128)S(1)}, f32[296,512]{1,0:T(8,128)S(1)}, u32[]{:S(2)}, u32[]{:S(2)}) %collective-permute-start.8) | collective-permute-done | bytes 606240 | tf_op jit(solution)/shard_map/ppermute | solution.py:545
  493.4 12.9 %collective-permute-done.9 = f32[296,512]{1,0:T(8,128)S(1)} collective-permute-done((f32[296,512]{1,0:T(8,128)S(1)}, f32[296,512]{1,0:T(8,128)S(1)}, u32[]{:S(2)}, u32[]{:S(2)}) %collective-permute-start.9) | collective-permute-done | bytes 606240 | tf_op jit(solution)/shard_map/ppermute | solution.py:545
  506.4 3.4 copy-done.7
  509.7 56.2 %stage.1 = (f32[8,8,64,512]{3,2,1,0:T(8,128)S(1)}, f32[8,8,64,512]{3,2,1,0:T(8,128)S(1)}) custom-call(s32[8]{0:T(128)S(1)} %stack.75.order_ref, f32[72]{0:T(128)S(1)} %dynamic_slice.94.jacobian_ref, f32[8,3,512]{2,1,0:T(4,128)S(1)} %maximum_bitcast_fusion.velocity_ref, bf16[192,192]{1,0:T(8,128)(2,1)S(1)} %copy-done.9, bf16[64,640]{1,0:T(8,128)(2,1)S(1)} %copy-done.10, ...), custom_call_target="tpu_custom_call" | custom-call | flops 5662310400 | bytes 38404096 | tf_op jit(solution)/shard_map/stage/pallas_call | solution.py:394
  566.0 42.2 %collide.3 = f32[8,512,512]{2,1,0:T(8,128)S(1)} custom-call(s32[192]{0:T(256)S(1)} %reshape.436.column_ref, f32[8,512,512]{2,1,0:T(8,128)S(1)} %bitcast.120, f32[8,512,512]{2,1,0:T(8,128)S(1)} %bitcast.121, f32[8,512,512]{2,1,0:T(8,128)S(1)} %bitcast.122, f32[8,512,512]{2,1,0:T(8,128)S(1)} %bitcast.123, f32[8,512,512]{2,1,0:T(8,128)S(1)} %bitcast.124, ...), custom_call_target="tpu_custom_call" | custom-call | flops 19327352832 | bytes 79691776 | tf_op jit(solution)/shard_map/collide/pallas_call | solution.py:472
  608.2 3.3 copy-done.4
  611.5 15.9 %faces.3 = (f32[384,16,512]{2,1,0:T(8,128)}, f32[48,16,512]{2,1,0:T(8,128)S(1)}, f32[48,16,512]{2,1,0:T(8,128)S(1)}, f32[48,16,512]{2,1,0:T(8,128)S(1)}) custom-call(s32[144]{0:T(256)S(1)} %pad_add_fusion.send_ref, f32[64,64,512]{2,1,0:T(8,128)} %copy-done.3, f32[64,56,512]{2,1,0:T(8,128)} %bitcast.33.refs_1_), custom_call_target="tpu_custom_call" | custom-call | bytes 66060288 | tf_op jit(solution)/shard_map/faces/pallas_call | solution.py:258
  634.3 28.6 %collective-permute-done.10 = f32[48,16,512]{2,1,0:T(8,128)S(1)} collective-permute-done((f32[48,16,512]{2,1,0:T(8,128)S(1)}, f32[48,16,512]{2,1,0:T(8,128)S(1)}, u32[]{:S(2)}, u32[]{:S(2)}) %collective-permute-start.10) | collective-permute-done | bytes 1572896 | tf_op jit(solution)/shard_map/ppermute | solution.py:587
  662.9 34.6 %collective-permute-done.11 = f32[48,16,512]{2,1,0:T(8,128)S(1)} collective-permute-done((f32[48,16,512]{2,1,0:T(8,128)S(1)}, f32[48,16,512]{2,1,0:T(8,128)S(1)}, u32[]{:S(2)}, u32[]{:S(2)}) %collective-permute-start.11) | collective-permute-done | bytes 1572896 | tf_op jit(solution)/shard_map/ppermute | solution.py:587
  697.5 4.1 collective-permute-start.17
  702.3 4.6 copy-done.5
  706.8 17.5 %inflow.3 = f32[64,64,512]{2,1,0:T(8,128)} custom-call(s32[384]{0:T(512)S(1)} %compare_select_fusion.2.lookup_ref, f32[576]{0:T(1024)S(1)} %reshape.435.jacobian_ref, f32[3,512]{1,0:T(4,128)S(1)} %pad_maximum_fusion.2.velocity_ref, bf16[64,192]{1,0:T(8,128)(2,1)S(1)} %copy-done.11, f32[384,16,512]{2,1,0:T(8,128)S(1)} %copy-done.5, ...), custom_call_target="tpu_custom_call" | custom-call | bytes 51380224 | tf_op jit(solution)/shard_map/inflow/pallas_call | solution.py:313
  739.3 69.6 %collective-permute-done.16 = f32[512,512]{1,0:T(8,128)S(1)} collective-permute-done((f32[512,512]{1,0:T(8,128)}, f32[512,512]{1,0:T(8,128)S(1)}, u32[]{:S(2)}, u32[]{:S(2)}) %collective-permute-start.16) | collective-permute-done | bytes 1048608 | tf_op jit(solution)/shard_map/ppermute | solution.py:545
  811.4 19.9 %collective-permute-done.17 = f32[512,512]{1,0:T(8,128)S(1)} collective-permute-done((f32[512,512]{1,0:T(8,128)S(1)}, f32[512,512]{1,0:T(8,128)S(1)}, u32[]{:S(2)}, u32[]{:S(2)}) %collective-permute-start.17) | collective-permute-done | bytes 1048608 | tf_op jit(solution)/shard_map/ppermute | solution.py:545
  833.8 23.0 %collective-permute-done.18 = f32[512,512]{1,0:T(8,128)S(1)} collective-permute-done((f32[512,512]{1,0:T(8,128)S(1)}, f32[512,512]{1,0:T(8,128)S(1)}, u32[]{:S(2)}, u32[]{:S(2)}) %collective-permute-start.18) | collective-permute-done | bytes 1048608 | tf_op jit(solution)/shard_map/ppermute | solution.py:545
  859.2 20.7 %collective-permute-done.19 = f32[512,512]{1,0:T(8,128)S(1)} collective-permute-done((f32[512,512]{1,0:T(8,128)S(1)}, f32[512,512]{1,0:T(8,128)S(1)}, u32[]{:S(2)}, u32[]{:S(2)}) %collective-permute-start.19) | collective-permute-done | bytes 1048608 | tf_op jit(solution)/shard_map/ppermute | solution.py:545
  (115 shorter events, 52.6 us)
Async XLA Ops:
  0.0 21.2 %copy-start = (f32[64,64]{1,0:T(8,128)S(1)}, f32[64,64]{1,0:T(8,128)}, u32[]{:S(2)}) copy-start(f32[64,64]{1,0:T(8,128)} %param.13) | copy-start | bytes 49156
  0.0 185.7 %all-to-all-start = ((f32[8,512,512]{2,1,0:T(8,128)}), f32[8,512,512]{2,1,0:T(8,128)}, u32[]{:S(2)}, u32[]{:S(2)}) async-start(f32[8,512,512]{2,1,0:T(8,128)} %bitcast.126), calls=%async_computation | async-start | bytes 16777216 | tf_op jit(solution)/shard_map/all_to_all | solution.py:581
  18.6 35.9 %collective-permute-start = (f32[48,16,512]{2,1,0:T(8,128)}, f32[48,16,512]{2,1,0:T(8,128)S(1)}, u32[]{:S(2)}, u32[]{:S(2)}) collective-permute-start(f32[48,16,512]{2,1,0:T(8,128)} %get-tuple-element.44), channel_id=1, source_target_pairs={{0,8},{8,0},{16,24},{24,16},{1,9},{9,1},{17,25},{25,17},{2,10},{10... | collective-permute-start | bytes 4718600 | tf_op jit(solution)/shard_map/ppermute | solution.py:587
  19.8 69.3 %collective-permute-start.1 = (f32[48,16,512]{2,1,0:T(8,128)}, f32[48,16,512]{2,1,0:T(8,128)}, u32[]{:S(2)}, u32[]{:S(2)}) collective-permute-start(f32[48,16,512]{2,1,0:T(8,128)} %get-tuple-element.45), channel_id=1, source_target_pairs={{0,16},{8,24},{16,0},{24,8},{1,17},{9,25},{17,1},{25,9},{2,18},{10... | collective-permute-start | bytes 4718600 | tf_op jit(solution)/shard_map/ppermute | solution.py:587
  20.0 69.1 %collective-permute-start.2 = (f32[48,16,512]{2,1,0:T(8,128)S(1)}, f32[48,16,512]{2,1,0:T(8,128)}, u32[]{:S(2)}, u32[]{:S(2)}) collective-permute-start(f32[48,16,512]{2,1,0:T(8,128)S(1)} %get-tuple-element.46), channel_id=1, source_target_pairs={{0,24},{8,16},{16,8},{24,0},{1,25},{9,17},{17,9},{25,1},{2,26},{10... | collective-permute-start | bytes 4718600 | tf_op jit(solution)/shard_map/ppermute | solution.py:587
  21.8 70.3 %copy-start.12 = (bf16[40,384]{1,0:T(8,128)(2,1)S(1)}, bf16[40,384]{1,0:T(8,128)(2,1)}, u32[]{:S(2)}) copy-start(bf16[40,384]{1,0:T(8,128)(2,1)} %constant.251.clone.lift_ref) | copy-start | bytes 92164
  89.1 24.4 %slice-start = ((s8[8388608]{0:T(1024)(128)(4,1)}), s8[4194304]{0:T(1024)(128)(4,1)S(1)}, s32[]{:S(2)}) async-start(s8[8388608]{0:T(1024)(128)(4,1)} %bitcast.127), calls=%async_computation.2 | async-start | bytes 8388608
  92.1 21.4 %slice-start.1 = ((s8[8388608]{0:T(1024)(128)(4,1)}), s8[4194304]{0:T(1024)(128)(4,1)S(1)}, s32[]{:S(2)}) async-start(s8[8388608]{0:T(1024)(128)(4,1)} %bitcast.127), calls=%async_computation.3 | async-start | bytes 8388608
  92.1 21.4 %copy-start.9 = (bf16[192,192]{1,0:T(8,128)(2,1)S(1)}, bf16[192,192]{1,0:T(8,128)(2,1)}, u32[]{:S(2)}) copy-start(bf16[192,192]{1,0:T(8,128)(2,1)} %constant.249.clone.derivative_ref) | copy-start | bytes 221188
  92.1 21.4 %copy-start.10 = (bf16[64,640]{1,0:T(8,128)(2,1)S(1)}, bf16[64,640]{1,0:T(8,128)(2,1)}, u32[]{:S(2)}) copy-start(bf16[64,640]{1,0:T(8,128)(2,1)} %constant.252.clone.spread_ref) | copy-start | bytes 245764
  234.9 376.6 %all-to-all-start.1 = ((f32[8,448,512]{2,1,0:T(8,128)}), f32[8,448,512]{2,1,0:T(8,128)}, u32[]{:S(2)}, u32[]{:S(2)}) async-start(f32[8,448,512]{2,1,0:T(8,128)} %copy-done.8), calls=%async_computation.1 | async-start | bytes 14680064 | tf_op jit(solution)/shard_map/all_to_all | solution.py:581
  247.7 2.4 collective-permute-start.3
  250.0 126.8 %collective-permute-start.4 = (f32[296,512]{1,0:T(8,128)}, f32[296,512]{1,0:T(8,128)S(1)}, u32[]{:S(2)}, u32[]{:S(2)}) collective-permute-start(f32[296,512]{1,0:T(8,128)} %get-tuple-element.59), channel_id=1, source_target_pairs={{0,2},{1,3},{2,0},{3,1},{4,6},{5,7},{6,4},{7,5},{8,10},{9,11},{10,... | collective-permute-start | bytes 1818632 | tf_op jit(solution)/shard_map/ppermute | solution.py:545
  252.0 138.8 %collective-permute-start.5 = (f32[296,512]{1,0:T(8,128)}, f32[296,512]{1,0:T(8,128)S(1)}, u32[]{:S(2)}, u32[]{:S(2)}) collective-permute-start(f32[296,512]{1,0:T(8,128)} %get-tuple-element.60), channel_id=1, source_target_pairs={{0,3},{1,2},{2,1},{3,0},{4,7},{5,6},{6,5},{7,4},{8,11},{9,10},{10,... | collective-permute-start | bytes 1818632 | tf_op jit(solution)/shard_map/ppermute | solution.py:545
  252.9 213.1 %collective-permute-start.6 = (f32[296,512]{1,0:T(8,128)S(1)}, f32[296,512]{1,0:T(8,128)S(1)}, u32[]{:S(2)}, u32[]{:S(2)}) collective-permute-start(f32[296,512]{1,0:T(8,128)S(1)} %get-tuple-element.61), channel_id=1, source_target_pairs={{0,4},{1,5},{2,6},{3,7},{4,0},{5,1},{6,2},{7,3},{8,12},{9,13},{10,... | collective-permute-start | bytes 1818632 | tf_op jit(solution)/shard_map/ppermute | solution.py:545
  253.0 226.0 %collective-permute-start.7 = (f32[296,512]{1,0:T(8,128)S(1)}, f32[296,512]{1,0:T(8,128)S(1)}, u32[]{:S(2)}, u32[]{:S(2)}) collective-permute-start(f32[296,512]{1,0:T(8,128)S(1)} %get-tuple-element.62), channel_id=1, source_target_pairs={{0,5},{1,4},{2,7},{3,6},{4,1},{5,0},{6,3},{7,2},{8,13},{9,12},{10,... | collective-permute-start | bytes 1818632 | tf_op jit(solution)/shard_map/ppermute | solution.py:545
  255.4 237.9 %collective-permute-start.8 = (f32[296,512]{1,0:T(8,128)S(1)}, f32[296,512]{1,0:T(8,128)S(1)}, u32[]{:S(2)}, u32[]{:S(2)}) collective-permute-start(f32[296,512]{1,0:T(8,128)S(1)} %get-tuple-element.63), channel_id=1, source_target_pairs={{0,6},{1,7},{2,4},{3,5},{4,2},{5,3},{6,0},{7,1},{8,14},{9,15},{10,... | collective-permute-start | bytes 1818632 | tf_op jit(solution)/shard_map/ppermute | solution.py:545
  376.8 129.5 %collective-permute-start.9 = (f32[296,512]{1,0:T(8,128)S(1)}, f32[296,512]{1,0:T(8,128)S(1)}, u32[]{:S(2)}, u32[]{:S(2)}) collective-permute-start(f32[296,512]{1,0:T(8,128)S(1)} %get-tuple-element.64), channel_id=1, source_target_pairs={{0,7},{1,6},{2,5},{3,4},{4,3},{5,2},{6,1},{7,0},{8,15},{9,14},{10,... | collective-permute-start | bytes 1818632 | tf_op jit(solution)/shard_map/ppermute | solution.py:545
  611.5 18.5 %slice-start.2 = ((s8[8388608]{0:T(1024)(128)(4,1)}), s8[4194304]{0:T(1024)(128)(4,1)S(1)}, s32[]{:S(2)}) async-start(s8[8388608]{0:T(1024)(128)(4,1)} %bitcast.129), calls=%async_computation.4 | async-start | bytes 8388608
  611.5 18.5 %slice-start.3 = ((s8[8388608]{0:T(1024)(128)(4,1)}), s8[4194304]{0:T(1024)(128)(4,1)S(1)}, s32[]{:S(2)}) async-start(s8[8388608]{0:T(1024)(128)(4,1)} %bitcast.129), calls=%async_computation.5 | async-start | bytes 8388608
  627.4 35.6 %collective-permute-start.10 = (f32[48,16,512]{2,1,0:T(8,128)S(1)}, f32[48,16,512]{2,1,0:T(8,128)S(1)}, u32[]{:S(2)}, u32[]{:S(2)}) collective-permute-start(f32[48,16,512]{2,1,0:T(8,128)S(1)} %get-tuple-element.70), channel_id=1, source_target_pairs={{0,8},{8,0},{16,24},{24,16},{1,9},{9,1},{17,25},{25,17},{2,10},{10... | collective-permute-start | bytes 4718600 | tf_op jit(solution)/shard_map/ppermute | solution.py:587
  628.6 68.9 %collective-permute-start.11 = (f32[48,16,512]{2,1,0:T(8,128)S(1)}, f32[48,16,512]{2,1,0:T(8,128)S(1)}, u32[]{:S(2)}, u32[]{:S(2)}) collective-permute-start(f32[48,16,512]{2,1,0:T(8,128)S(1)} %get-tuple-element.71), channel_id=1, source_target_pairs={{0,16},{8,24},{16,0},{24,8},{1,17},{9,25},{17,1},{25,9},{2,18},{10... | collective-permute-start | bytes 4718600 | tf_op jit(solution)/shard_map/ppermute | solution.py:587
  628.8 68.7 %collective-permute-start.12 = (f32[48,16,512]{2,1,0:T(8,128)S(1)}, f32[48,16,512]{2,1,0:T(8,128)S(1)}, u32[]{:S(2)}, u32[]{:S(2)}) collective-permute-start(f32[48,16,512]{2,1,0:T(8,128)S(1)} %get-tuple-element.72), channel_id=1, source_target_pairs={{0,24},{8,16},{16,8},{24,0},{1,25},{9,17},{17,9},{25,1},{2,26},{10... | collective-permute-start | bytes 4718600 | tf_op jit(solution)/shard_map/ppermute | solution.py:587
  633.0 69.2 %copy-start.11 = (bf16[64,192]{1,0:T(8,128)(2,1)S(1)}, bf16[64,192]{1,0:T(8,128)(2,1)}, u32[]{:S(2)}) copy-start(bf16[64,192]{1,0:T(8,128)(2,1)} %constant.250.clone.lift_ref) | copy-start | bytes 73732
  633.0 95.0 %collective-permute-start.13 = (f32[512,512]{1,0:T(8,128)}, f32[512,512]{1,0:T(8,128)}, u32[]{:S(2)}, u32[]{:S(2)}) collective-permute-start(f32[512,512]{1,0:T(8,128)} %get-tuple-element.74), channel_id=1, source_target_pairs={{0,1},{1,0},{2,3},{3,2},{4,5},{5,4},{6,7},{7,6},{8,9},{9,8},{10,11... | collective-permute-start | bytes 3145736 | tf_op jit(solution)/shard_map/ppermute | solution.py:545
  634.3 98.8 %collective-permute-start.14 = (f32[512,512]{1,0:T(8,128)}, f32[512,512]{1,0:T(8,128)}, u32[]{:S(2)}, u32[]{:S(2)}) collective-permute-start(f32[512,512]{1,0:T(8,128)} %get-tuple-element.75), channel_id=1, source_target_pairs={{0,2},{1,3},{2,0},{3,1},{4,6},{5,7},{6,4},{7,5},{8,10},{9,11},{10,... | collective-permute-start | bytes 3145736 | tf_op jit(solution)/shard_map/ppermute | solution.py:545
  662.9 73.9 %collective-permute-start.15 = (f32[512,512]{1,0:T(8,128)}, f32[512,512]{1,0:T(8,128)S(1)}, u32[]{:S(2)}, u32[]{:S(2)}) collective-permute-start(f32[512,512]{1,0:T(8,128)} %get-tuple-element.76), channel_id=1, source_target_pairs={{0,3},{1,2},{2,1},{3,0},{4,7},{5,6},{6,5},{7,4},{8,11},{9,10},{10,... | collective-permute-start | bytes 3145736 | tf_op jit(solution)/shard_map/ppermute | solution.py:545
  697.5 111.4 %collective-permute-start.16 = (f32[512,512]{1,0:T(8,128)}, f32[512,512]{1,0:T(8,128)S(1)}, u32[]{:S(2)}, u32[]{:S(2)}) collective-permute-start(f32[512,512]{1,0:T(8,128)} %get-tuple-element.77), channel_id=1, source_target_pairs={{0,4},{1,5},{2,6},{3,7},{4,0},{5,1},{6,2},{7,3},{8,12},{9,13},{10,... | collective-permute-start | bytes 3145736 | tf_op jit(solution)/shard_map/ppermute | solution.py:545
  697.5 133.8 %collective-permute-start.17 = (f32[512,512]{1,0:T(8,128)S(1)}, f32[512,512]{1,0:T(8,128)S(1)}, u32[]{:S(2)}, u32[]{:S(2)}) collective-permute-start(f32[512,512]{1,0:T(8,128)S(1)} %get-tuple-element.78), channel_id=1, source_target_pairs={{0,5},{1,4},{2,7},{3,6},{4,1},{5,0},{6,3},{7,2},{8,13},{9,12},{10,... | collective-permute-start | bytes 3145736 | tf_op jit(solution)/shard_map/ppermute | solution.py:545
  728.1 128.7 %collective-permute-start.18 = (f32[512,512]{1,0:T(8,128)S(1)}, f32[512,512]{1,0:T(8,128)S(1)}, u32[]{:S(2)}, u32[]{:S(2)}) collective-permute-start(f32[512,512]{1,0:T(8,128)S(1)} %get-tuple-element.79), channel_id=1, source_target_pairs={{0,6},{1,7},{2,4},{3,5},{4,2},{5,3},{6,0},{7,1},{8,14},{9,15},{10,... | collective-permute-start | bytes 3145736 | tf_op jit(solution)/shard_map/ppermute | solution.py:545
  733.0 146.9 %collective-permute-start.19 = (f32[512,512]{1,0:T(8,128)S(1)}, f32[512,512]{1,0:T(8,128)S(1)}, u32[]{:S(2)}, u32[]{:S(2)}) collective-permute-start(f32[512,512]{1,0:T(8,128)S(1)} %get-tuple-element.80), channel_id=1, source_target_pairs={{0,7},{1,6},{2,5},{3,4},{4,3},{5,2},{6,1},{7,0},{8,15},{9,14},{10,... | collective-permute-start | bytes 3145736 | tf_op jit(solution)/shard_map/ppermute | solution.py:545
  831.3 49.8 %copy-start.1 = (f32[64,64]{1,0:T(8,128)S(1)}, f32[64,64]{1,0:T(8,128)}, u32[]{:S(2)}) copy-start(f32[64,64]{1,0:T(8,128)} %param.13) | copy-start | bytes 49156
  (11 other events, 76.6 us)
